TPU v7x, 128 devices: a whole 4x4x4 slice. The times are simulated.
128 devices in a mesh: gz: 16 (over z, y), gy: 8 (over x, core).
Axes of the slice: x: 4, y: 4, z: 4, core: 2. Of those that a mesh axis runs over, the one named last changes fastest.
Arguments:
- species_field: float32 [4, 512, 512, 512], P(None, 'gz', 'gy'), may hold values from -100 to 100
Outputs:
- core_tensor: float32 [4, 512, 4096], P(None, ('gz', 'gy'))
- basis_z: float32 [512, 64], replicated
- basis_y: float32 [512, 64], replicated
All inputs are finite; a program needn't handle non-finite values.
Results may differ from a plain program's by a relative error of at most 0.0003.
Values sent between devices are 32-bit elements; how exact they have to be, the bound alone decides.
A program may use at most 192 MiB of HBM per device.

v0:
```python
import math
import jax
import jax.numpy as jnp
from jax import lax
from jax.sharding import PartitionSpec as P

GRID = 512
RANK = 64
ITERS = 4


def start_table(order, width):
    row_index = jnp.arange(order).astype(jnp.float32)
    col_index = jnp.arange(width).astype(jnp.float32)
    return jnp.cos(math.pi * (row_index[:, None] + 0.5) * col_index[None, :] / order)


def solve_factor(product, inner_gram):
    factor = jnp.linalg.cholesky(inner_gram)
    return lax.linalg.triangular_solve(
        factor, product, left_side=False, lower=True, transpose_a=True
    )


def inner_products(left, right):
    return lax.dot_general(left, right, (((0,), (0,)), ((), ())), precision=lax.Precision.HIGHEST)


def mode_products(left, right, mode):
    others = tuple((d for d in range(4) if d != mode))
    return lax.dot_general(
        left, right, ((others, others), ((), ())), precision=lax.Precision.HIGHEST
    )


def leaf_basis(fibres, mode):
    basis_now = start_table(GRID, RANK)
    gram_total = lax.psum(mode_products(fibres, fibres, mode), ("gz", "gy"))
    for iteration in range(ITERS):
        product = jnp.dot(gram_total, basis_now, precision=lax.Precision.HIGHEST)
        basis_now = solve_factor(product, inner_products(product, product))
    return basis_now


def body(species_field):
    fibres_z = lax.all_to_all(species_field, "gz", split_axis=2, concat_axis=1, tiled=True)
    basis_z = leaf_basis(fibres_z, 1)
    reduced = jnp.einsum("szyx,zr->sryx", fibres_z, basis_z, precision=lax.Precision.HIGHEST)
    mixed = lax.all_to_all(reduced, ("gz", "gy"), split_axis=3, concat_axis=2, tiled=True)
    count_gz = lax.axis_size("gz")
    count_gy = lax.axis_size("gy")
    shape_now = mixed.shape
    y_local = shape_now[2] // (count_gz * count_gy)
    blocks = mixed.reshape(shape_now[0], shape_now[1], count_gz, count_gy, y_local, shape_now[3])
    fibres_y = jnp.transpose(blocks, (0, 1, 3, 2, 4, 5)).reshape(shape_now)
    basis_y = leaf_basis(fibres_y, 2)
    core_tensor = jnp.einsum("sryx,yq->sxrq", fibres_y, basis_y, precision=lax.Precision.HIGHEST)
    core_tensor = core_tensor.reshape(fibres_y.shape[0], fibres_y.shape[3], RANK * RANK)
    return (core_tensor, basis_z, basis_y)


def solution(mesh):
    in_specs = (P(None, "gz", "gy", None),)
    out_specs = (P(None, ("gz", "gy"), None), P(), P())
    return jax.shard_map(body, mesh=mesh, in_specs=in_specs, out_specs=out_specs, check_vma=False)
```

profile of v0, /device:TPU:1, one launch (start us, length us, event | category | flops | bytes accessed | tf_op | source)
XLA Modules:
  0.0 767.0 jit_solution(3029973958028382066)
XLA Ops:
  7.2 15.2 %copy.29 = f32[4,32,64,512]{3,1,0,2:T(8,128)S(1)} copy(f32[4,32,64,512]{3,2,1,0:T(8,128)} %param.4) | data formatting | bytes 33554432 | tf_op args[0]
  22.5 193.2 %all_to_all.33 = f32[4,32,64,512]{3,1,0,2:T(8,128)} all-to-all(f32[4,32,64,512]{3,1,0,2:T(8,128)S(1)} %copy.29), channel_id=1, replica_groups=mesh['gz'=16,'gy'=8] {'gz'}, dimensions={2} | all-to-all | bytes 33554432 | tf_op jit(solution)/shard_map/all_to_all | solution.py:46
  215.6 6.9 copy.30
  222.5 5.7 copy-done
  228.2 28.8 %convolution_bitcast_fusion.2 = f32[512,512]{1,0:T(8,128)} fusion(f32[4,512,4,512]{3,1,2,0:T(8,128)S(1)} %bitcast.170), kind=kOutput, calls=%fused_computation.2 | convolution fusion | flops 25769803776 | bytes 17825792 | tf_op jit(solution)/shard_map/dot_general | solution.py:31
  257.3 146.0 %all-reduce.3.cloned.1.call-done = f32[512,512]{1,0:T(8,128)} async-done(((f32[512,512]{1,0:T(8,128)}), f32[512,512]{1,0:T(8,128)}) %all-reduce.3.cloned.1.call-update) | async-done | bytes 1048592 | tf_op jit(solution)/shard_map/psum | solution.py:38
  403.3 3.4 fusion.1
  407.0 5.8 cholesky.134
  413.6 0.7 fusion.10
  414.2 4.9 custom-call.12
  419.5 2.4 fusion.53
  422.2 5.8 cholesky.145
  428.7 0.7 fusion.11
  429.4 4.9 custom-call.13
  434.6 1.1 fusion.55
  436.1 5.8 cholesky.156
  442.7 0.7 fusion.12
  443.3 4.9 custom-call.14
  448.6 1.1 fusion.57
  450.1 5.8 cholesky.167
  456.6 1.0 fusion.13
  457.6 4.9 custom-call.15
  462.8 14.2 %convolution_bitcast_fusion = f32[4,64,4,512]{3,1,2,0:T(8,128)S(1)} fusion(f32[4,512,4,512]{3,1,2,0:T(8,128)} %bitcast.171, f32[64,512]{1,0:T(8,128)S(1)} %fusion.27), kind=kOutput, calls=%fused_computation | convolution fusion | flops 3221225472 | bytes 19005440 | tf_op jit(solution)/shard_map/szyx,zr->sryx/dot_general | solution.py:48
  477.1 3.4 copy.35
  480.5 5.3 reshape.76
  485.8 37.2 %all_to_all.34 = f32[128,1,4096]{2,1,0:T(1,128)} all-to-all(f32[128,1,4096]{2,1,0:T(1,128)S(1)} %reshape.76), channel_id=1, replica_groups=mesh['gz'=16,'gy'=8] {'gz','gy'}, dimensions={0} | all-to-all | bytes 4194304 | tf_op jit(solution)/shard_map/all_to_all | solution.py:49
  523.6 7.3 reduce.4
  530.9 4.3 reshape.77
  535.2 3.5 copy.36
  538.8 2.7 copy.37
  541.5 1.9 copy-done.1
  543.4 8.0 %convolution_bitcast_fusion.1 = f32[512,512]{1,0:T(8,128)} fusion(f32[4,64,512,4]{1,2,3,0:T(8,128)S(1)} %bitcast.172), kind=kOutput, calls=%fused_computation.1 | convolution fusion | flops 3221225472 | bytes 3145728 | tf_op jit(solution)/shard_map/dot_general | solution.py:31
  551.4 143.0 %all-reduce.5.cloned.1.call-done = f32[512,512]{1,0:T(8,128)} async-done(((f32[512,512]{1,0:T(8,128)}), f32[512,512]{1,0:T(8,128)}) %all-reduce.5.cloned.1.call-update) | async-done | bytes 1048592 | tf_op jit(solution)/shard_map/psum | solution.py:38
  694.4 3.6 fusion
  698.4 5.8 cholesky.178
  705.5 4.9 custom-call.16
  710.8 2.4 fusion.60
  713.5 5.8 cholesky.189
  720.0 0.7 fusion.15
  720.7 4.9 custom-call.17
  725.9 1.1 fusion.62
  727.4 5.8 cholesky.200
  734.6 4.9 custom-call.18
  739.9 1.1 fusion.64
  741.4 5.8 cholesky.211
  748.5 4.9 custom-call.19
  753.8 4.9 convolution_bitcast_fusion.3
  758.9 0.9 reshape.41
  (69 shorter events, 13.8 us)
Async XLA Ops:
  7.2 396.1 %all-reduce.3.cloned.1.call-start = ((), (), s32[]{:S(2)}) async-start(), calls=%async_computation.2 | async-start | bytes 2097152 | tf_op jit(solution)/shard_map/psum | solution.py:38
  222.5 5.7 copy-start
  257.0 437.4 %all-reduce.5.cloned.1.call-start = ((), (), s32[]{:S(2)}) async-start(), calls=%async_computation.3 | async-start | bytes 2097152 | tf_op jit(solution)/shard_map/psum | solution.py:38
  403.3 31.3 %copy-start.2 = (f32[512,512]{1,0:T(8,128)S(1)}, f32[512,512]{1,0:T(8,128)}, u32[]{:S(2)}) copy-start(f32[512,512]{1,0:T(8,128)} %all-reduce.3.cloned.1.call-done) | copy-start | bytes 3145732
  462.8 14.2 %copy-start.4 = (f32[64,512]{1,0:T(8,128)}, f32[64,512]{1,0:T(8,128)S(1)}, u32[]{:S(2)}) copy-start(f32[64,512]{1,0:T(8,128)S(1)} %fusion.27) | copy-start | bytes 393220
  541.5 1.9 copy-start.1
  694.4 31.5 %copy-start.3 = (f32[512,512]{1,0:T(8,128)S(1)}, f32[512,512]{1,0:T(8,128)}, u32[]{:S(2)}) copy-start(f32[512,512]{1,0:T(8,128)} %all-reduce.5.cloned.1.call-done) | copy-start | bytes 3145732
  753.8 6.0 copy-start.5
Sparse Core Ops, SparseCore 0:
  257.1 146.1 all-reduce.2
  551.5 142.8 all-reduce.4
where the time goes:
time: 776 us; the launch traced here: 767 us
  waiting for transfers between devices  289 us (37%)
  blocking collectives  230 us (30%)
  other arithmetic  104 us (13%)
  matrix products  76.8 us (10%)
  local copies, waits for them, and re-layouts  51.3 us (7%)
  between operations  14.9 us (2%)
    psum x2, waiting for transfers between devices, leaf_basis(): gram_total = lax.psum(mode_products(fibres, fibres, mode), ('gz', 'gy'))  289 us
    all_to_all x1, blocking collectives, body(): lax.all_to_all(species_field, 'gz', split_axis=2, concat_axis=1, tiled=True)  193 us
    another operation x24, other arithmetic, solve_factor(): factor = jnp.linalg.cholesky(inner_gram)  52.2 us
    another operation x16, other arithmetic, solve_factor(): lax.linalg.triangular_solve(factor, product, left_side=False, lower=True,...  44.7 us
    all_to_all x1, blocking collectives, body(): lax.all_to_all(reduced, ('gz', 'gy'), split_axis=3, concat_axis=2, tiled=...  37.2 us
    dot_general x2, matrix products, mode_products(): lax.dot_general(left, right, ((others, others), ((), ())), precision=lax....  36.7 us
    unnamed x15, local copies, waits for them, and re-layouts  32.5 us
    dot_general x8, matrix products, leaf_basis(): product = jnp.dot(gram_total, basis_now, precision=lax.Precision.HIGHEST)  16.2 us
  transfers between devices with their start and end apart: 2, of which 2 were waited for; matrix products, arithmetic and copies ran while one was open for 0% of the time, Pallas kernels for 0%

commit v1 on v0

--- a/solution.py
+++ b/solution.py
@@ -35,7 +35,7 @@
 
 def leaf_basis(fibres, mode):
     basis_now = start_table(GRID, RANK)
-    gram_total = lax.psum(mode_products(fibres, fibres, mode), ("gz", "gy"))
+    gram_total = jnp.sum(lax.all_gather(mode_products(fibres, fibres, mode), ("gz", "gy")), axis=0)
     for iteration in range(ITERS):
         product = jnp.dot(gram_total, basis_now, precision=lax.Precision.HIGHEST)
         basis_now = solve_factor(product, inner_products(product, product))

time: 776 us -> 1130 us (1.46)
  waiting for transfers between devices: 289 us -> 562 us
  other arithmetic: 104 us -> 186 us
    all_gather x0 -> x2, waiting for transfers between devices: none -> 562 us  [leaf_basis(): lax.all_gather(mode_products(fibres, fibres, mode), ('gz', 'gy'))]
    psum x2 -> x0, waiting for transfers between devices: 289 us -> none  [leaf_basis(): gram_total = lax.psum(mode_products(fibres, fibres, mode), ('gz', 'gy'))]
    reduce_sum x0 -> x2, other arithmetic: none -> 81.5 us  [leaf_basis(): jnp.sum(lax.all_gather(mode_products(fibres, fibres, mode), ('gz', 'gy'))...]
    unnamed x15 -> x11, local copies, waits for them, and re-layouts: 32.5 us -> 32.5 us
where the time goes in v1:
time: 1130 us; the launch traced here: 1120 us
  waiting for transfers between devices  562 us (50%)
  blocking collectives  230 us (20%)
  other arithmetic  186 us (16%)
  matrix products  71.5 us (6%)
  local copies, waits for them, and re-layouts  51.3 us (5%)
  between operations  14.9 us (1%)
    all_gather x2, waiting for transfers between devices, leaf_basis(): lax.all_gather(mode_products(fibres, fibres, mode), ('gz', 'gy'))  562 us
    all_to_all x1, blocking collectives, body(): lax.all_to_all(species_field, 'gz', split_axis=2, concat_axis=1, tiled=True)  193 us
    reduce_sum x2, other arithmetic, leaf_basis(): jnp.sum(lax.all_gather(mode_products(fibres, fibres, mode), ('gz', 'gy'))...  81.5 us
    another operation x24, other arithmetic, solve_factor(): factor = jnp.linalg.cholesky(inner_gram)  52.2 us
    another operation x16, other arithmetic, solve_factor(): lax.linalg.triangular_solve(factor, product, left_side=False, lower=True,...  44.9 us
    all_to_all x1, blocking collectives, body(): lax.all_to_all(reduced, ('gz', 'gy'), split_axis=3, concat_axis=2, tiled=...  37.2 us
    dot_general x2, matrix products, mode_products(): lax.dot_general(left, right, ((others, others), ((), ())), precision=lax....  36.6 us
    unnamed x11, local copies, waits for them, and re-layouts  32.5 us
  transfers between devices with their start and end apart: 2, of which 2 were waited for; matrix products, arithmetic and copies ran while one was open for 0% of the time, Pallas kernels for 0%

profile of v1, /device:TPU:1, one launch (start us, length us, event | category | flops | bytes accessed | tf_op | source)
XLA Modules:
  0.0 1116.3 jit_solution(7040446045665915288)
XLA Ops:
  7.2 15.2 %copy.29 = f32[4,32,64,512]{3,1,0,2:T(8,128)S(1)} copy(f32[4,32,64,512]{3,2,1,0:T(8,128)} %param.4) | data formatting | bytes 33554432 | tf_op args[0]
  22.5 193.2 %all_to_all.33 = f32[4,32,64,512]{3,1,0,2:T(8,128)} all-to-all(f32[4,32,64,512]{3,1,0,2:T(8,128)S(1)} %copy.29), channel_id=1, replica_groups=mesh['gz'=16,'gy'=8] {'gz'}, dimensions={2} | all-to-all | bytes 33554432 | tf_op jit(solution)/shard_map/all_to_all | solution.py:46
  215.6 6.9 copy.30
  222.5 5.7 copy-done
  228.2 28.7 %convolution_bitcast_fusion.2 = f32[512,512]{1,0:T(8,128)} fusion(f32[4,512,4,512]{3,1,2,0:T(8,128)S(1)} %bitcast.172), kind=kOutput, calls=%fused_computation.2 | convolution fusion | flops 25769803776 | bytes 17825792 | tf_op jit(solution)/shard_map/dot_general | solution.py:31
  257.0 282.7 %all-gather.5.cloned.1.call-done = f32[65536,512]{1,0:T(8,128)} async-done(((f32[512,512]{1,0:T(8,128)}), f32[65536,512]{1,0:T(8,128)}) %all-gather.5.cloned.1.call-update) | async-done | bytes 134217744 | tf_op jit(solution)/shard_map/all_gather | solution.py:38
  539.8 40.7 %reduce_sum.18 = f32[512,512]{1,0:T(8,128)S(1)} reduce(f32[128,512,512]{2,1,0:T(8,128)} %bitcast.5, f32[]{:T(128)} %constant.34.clone.1), dimensions={0}, to_apply=%region_0.0 | reduce | flops 33292288 | bytes 135266304 | tf_op jit(solution)/shard_map/reduce_sum | solution.py:38
  580.5 2.1 fusion.1
  582.9 5.8 cholesky.134
  589.5 0.7 fusion.10
  590.1 4.9 custom-call.12
  595.4 1.1 fusion.53
  596.9 5.8 cholesky.145
  603.4 0.7 fusion.11
  604.1 4.9 custom-call.13
  609.3 1.1 fusion.55
  610.8 5.8 cholesky.156
  617.3 0.7 fusion.12
  618.0 4.9 custom-call.14
  623.2 1.1 fusion.57
  624.7 5.8 cholesky.167
  631.9 5.2 custom-call.15
  637.5 14.2 %convolution_bitcast_fusion = f32[4,64,4,512]{3,1,2,0:T(8,128)S(1)} fusion(f32[4,512,4,512]{3,1,2,0:T(8,128)} %bitcast.173, f32[64,512]{1,0:T(8,128)S(1)} %fusion.27), kind=kOutput, calls=%fused_computation | convolution fusion | flops 3221225472 | bytes 19005440 | tf_op jit(solution)/shard_map/szyx,zr->sryx/dot_general | solution.py:48
  651.7 3.4 copy.35
  655.1 5.3 reshape.78
  660.5 37.2 %all_to_all.34 = f32[128,1,4096]{2,1,0:T(1,128)} all-to-all(f32[128,1,4096]{2,1,0:T(1,128)S(1)} %reshape.78), channel_id=1, replica_groups=mesh['gz'=16,'gy'=8] {'gz','gy'}, dimensions={0} | all-to-all | bytes 4194304 | tf_op jit(solution)/shard_map/all_to_all | solution.py:49
  698.2 7.3 reduce.4
  705.5 4.3 reshape.79
  709.8 3.5 copy.36
  713.3 2.7 copy.37
  716.1 1.9 copy-done.1
  718.0 7.9 convolution_bitcast_fusion.1
  725.9 279.5 %all-gather.7.cloned.1.call-done = f32[65536,512]{1,0:T(8,128)} async-done(((f32[512,512]{1,0:T(8,128)}), f32[65536,512]{1,0:T(8,128)}) %all-gather.7.cloned.1.call-update) | async-done | bytes 134217744 | tf_op jit(solution)/shard_map/all_gather | solution.py:38
  1005.5 40.8 %reduce_sum.19 = f32[512,512]{1,0:T(8,128)S(1)} reduce(f32[128,512,512]{2,1,0:T(8,128)} %bitcast.33, f32[]{:T(128)} %constant.34.clone.1), dimensions={0}, to_apply=%region_3.6 | reduce | flops 33292288 | bytes 135266304 | tf_op jit(solution)/shard_map/reduce_sum | solution.py:38
  1046.2 2.1 fusion
  1048.7 5.8 cholesky.178
  1055.8 4.9 custom-call.16
  1061.1 1.1 fusion.60
  1062.6 5.8 cholesky.189
  1069.8 4.9 custom-call.17
  1075.0 1.1 fusion.62
  1076.5 5.8 cholesky.200
  1083.7 4.9 custom-call.18
  1088.9 1.1 fusion.64
  1090.4 5.8 cholesky.211
  1097.6 5.1 custom-call.19
  1103.0 4.9 convolution_bitcast_fusion.3
  1108.1 0.9 reshape.41
  (67 shorter events, 14.9 us)
Async XLA Ops:
  7.2 532.6 %all-gather.5.cloned.1.call-start = ((), (), s32[]{:S(2)}) async-start(), calls=%async_computation.2 | async-start | bytes 135266304 | tf_op jit(solution)/shard_map/all_gather | solution.py:38
  222.5 5.7 copy-start
  257.0 748.5 %all-gather.7.cloned.1.call-start = ((), (), s32[]{:S(2)}) async-start(), calls=%async_computation.3 | async-start | bytes 135266304 | tf_op jit(solution)/shard_map/all_gather | solution.py:38
  637.5 14.2 %copy-start.2 = (f32[64,512]{1,0:T(8,128)}, f32[64,512]{1,0:T(8,128)S(1)}, u32[]{:S(2)}) copy-start(f32[64,512]{1,0:T(8,128)S(1)} %fusion.27) | copy-start | bytes 393220
  716.0 1.9 copy-start.1
  1103.0 6.0 copy-start.3
Sparse Core Ops, SparseCore 0:
  257.1 282.6 all-gather.4
  726.0 279.3 all-gather.6
